TPU v7x, 32 devices: a whole 2x2x4 slice. The times are simulated.
32 devices in a mesh: seq: 32 (over z, y, x, core).
Axes of the slice: x: 2, y: 2, z: 4, core: 2. Of those that a mesh axis runs over, the one named last changes fastest.
Arguments:
- block_input: float32 [4096, 1024], P('seq'), may hold values from -6 to 6
- cotangent: float32 [4096, 1024], P('seq'), may hold values from -6 to 6
- attn_gain: bfloat16 [1024], P('seq'), may hold values from 0.5 to 1.5
- w_query: bfloat16 [1024, 512], P('seq'), may hold values from -0.1875 to 0.1875
- w_key: bfloat16 [1024, 512], P('seq'), may hold values from -0.1875 to 0.1875
- w_value: bfloat16 [1024, 1024], P('seq'), may hold values from -0.1875 to 0.1875
- w_outgate: bfloat16 [1024, 1024], P('seq'), may hold values from -0.1875 to 0.1875
- w_decay_down: bfloat16 [1024, 16], P('seq'), may hold values from -0.1875 to 0.1875
- w_decay_up: bfloat16 [16, 512], P(None, 'seq'), may hold values from -2.5 to 2.5
- decay_bias: bfloat16 [512], P('seq')
- head_gain: bfloat16 [256], P('seq'), may hold values from 0.5 to 1.5
- w_out: bfloat16 [1024, 1024], P('seq'), may hold values from -0.1875 to 0.1875
- mlp_gain: bfloat16 [1024], P('seq'), may hold values from 0.5 to 1.5
- w_gate: bfloat16 [1024, 2816], P('seq'), may hold values from -0.1875 to 0.1875
- w_up: bfloat16 [1024, 2816], P('seq'), may hold values from -0.1875 to 0.1875
- w_down: bfloat16 [2816, 1024], P('seq'), may hold values from -0.109375 to 0.109375
Outputs:
- block_output: float32 [4096, 1024], P('seq')
- input_grad: float32 [4096, 1024], P('seq')
- grad_attn_gain: float32 [1024], P('seq')
- grad_query: float32 [1024, 512], P('seq')
- grad_key: float32 [1024, 512], P('seq')
- grad_value: float32 [1024, 1024], P('seq')
- grad_outgate: float32 [1024, 1024], P('seq')
- grad_decay_down: float32 [1024, 16], P('seq')
- grad_decay_up: float32 [16, 512], P(None, 'seq')
- grad_decay_bias: float32 [512], P('seq')
- grad_head_gain: float32 [256], P('seq')
- grad_out: float32 [1024, 1024], P('seq')
- grad_mlp_gain: float32 [1024], P('seq')
- grad_gate: float32 [1024, 2816], P('seq')
- grad_up: float32 [1024, 2816], P('seq')
- grad_down: float32 [2816, 1024], P('seq')
All inputs are finite; a program needn't handle non-finite values.
Results may differ from a plain program's by a relative error of at most 0.02.
Values may be sent and summed in bfloat16 or wider, within the bound.
No kernel may reach another device: no remote copies, remote signals or barrier semaphores. Data moves between devices by JAX's collectives and lax.ppermute only.
A program may use at most 320 MiB of HBM per device.

v0:
```python
import jax
import jax.numpy as jnp
from jax import lax
from jax.sharding import PartitionSpec as P

H = 4
DK = 128
VALUE_WIDTH = 256
GROUP = 64


EPS = 1e-05
GATE_NORM = 16.0
TOP_PRECISION = lax.Precision.HIGHEST


def carried_in(value, axis, join, neutral):
    count, mine = (lax.axis_size(axis), lax.axis_index(axis))
    pieces = jax.tree.map(lambda part: lax.all_gather(part, axis), value)
    subtotal = jax.tree.map(
        lambda part, zero: jnp.full_like(part, 0) + jnp.asarray(zero, part.dtype), value, neutral
    )

    def carried_hop(position, subtotal):
        longer = join(subtotal, jax.tree.map(lambda part: part[position], pieces))
        return jax.tree.map(lambda new, old: jnp.where(position < mine, new, old), longer, subtotal)

    return lax.fori_loop(0, count - 1, carried_hop, subtotal)


def entering(array, axis, combine, identity):
    devices, index = (lax.axis_size(axis), lax.axis_index(axis))
    everything = jax.tree.map(
        lambda part, kind: lax.all_gather(part.astype(kind), axis),
        array,
        jax.tree.map(lambda a: jnp.bfloat16 if a.dtype == jnp.float32 else a.dtype, array),
    )
    start = jax.tree.map(
        lambda part, zero: jnp.broadcast_to(jnp.asarray(zero, part.dtype), part.shape),
        array,
        identity,
    )

    def entering_hop(k, before):
        at = devices - 1 - k
        reached = at > index
        new = combine(
            before, jax.tree.map(lambda part, own: part[at].astype(own.dtype), everything, array)
        )
        return jax.tree.map(lambda a, b: jnp.where(reached, a, b), new, before)

    return lax.fori_loop(0, devices, entering_hop, start)


def matmul(left_side, right_side):
    return jnp.dot(left_side, right_side, preferred_element_type=jnp.float32)


def times_back(left_side, right_side):
    return lax.dot_general(
        left_side, right_side, (((1,), (1,)), ((), ())), preferred_element_type=jnp.float32
    )


def outer_sum(left_side, right_side):
    return lax.dot_general(
        left_side, right_side, (((0,), (0,)), ((), ())), preferred_element_type=jnp.float32
    )


def rms_norm(matrix, gain):
    scaling = lax.rsqrt(jnp.mean(matrix * matrix, axis=-1, keepdims=True) + EPS)
    return matrix * scaling * gain


def swiglu(gate_pre, up_pre):
    return jax.nn.silu(gate_pre) * up_pre


def split_into_heads(matrix, columns):
    return matrix.reshape(matrix.shape[0] // GROUP, GROUP, H, columns).transpose(2, 0, 1, 3)


def from_heads(blocks):
    return blocks.transpose(1, 2, 0, 3).reshape(
        blocks.shape[1] * blocks.shape[2], blocks.shape[0] * blocks.shape[3]
    )


def to_front(tensor):
    return jnp.moveaxis(tensor, 1, 0)


def group_pass(query_blocks, key_blocks, value_blocks, decay_blocks, initial):
    inner = jnp.cumsum(decay_blocks, axis=2)
    ending = inner[:, :, -1:, :]
    query_in = query_blocks * jnp.exp(inner)
    key_in = key_blocks * jnp.exp(-inner)
    key_end = key_blocks * jnp.exp(ending - inner)
    length = query_blocks.shape[2]
    causal = jnp.tril(jnp.ones((length, length), jnp.float32))
    scores = jnp.einsum("hnck,hnsk->hncs", query_in, key_in, precision=TOP_PRECISION) * causal
    within = jnp.einsum("hncs,hnsv->hncv", scores, value_blocks, precision=TOP_PRECISION)

    def advance(carried_state, sequence_segments):
        query_segment, key_segment, value_segment, fading_factor = sequence_segments
        block_result = jnp.einsum(
            "waq,wqo->wao", query_segment, carried_state, precision=TOP_PRECISION
        )
        carried_state = fading_factor[:, 0, :, None] * carried_state + jnp.einsum(
            "fjb,fjq->fbq", key_segment, value_segment, precision=TOP_PRECISION
        )
        return (carried_state, block_result)

    final, across_pieces = lax.scan(
        advance,
        initial,
        (to_front(query_in), to_front(key_end), to_front(value_blocks), to_front(jnp.exp(ending))),
    )
    return (within + to_front(across_pieces), final)


def post_gate(mixer, outgate, head_gain):
    tokens_here = mixer.shape[0]
    per_head = mixer.reshape(tokens_here, H, VALUE_WIDTH)
    normed = rms_norm(per_head, head_gain).reshape(tokens_here, H * VALUE_WIDTH)
    return normed * outgate * jax.nn.sigmoid(outgate)


def local_pass(query, keys, values, decay_logit):
    log_decay = jax.nn.log_sigmoid(decay_logit) / GATE_NORM
    query_blocks = split_into_heads(query, DK)
    decay_blocks = split_into_heads(log_decay, DK)
    zero_state = jnp.zeros((H, DK, VALUE_WIDTH), jnp.float32)
    local_out, local_state = group_pass(
        query_blocks,
        split_into_heads(keys, DK),
        split_into_heads(values, VALUE_WIDTH),
        decay_blocks,
        zero_state,
    )
    layout = decay_blocks.shape
    cumulative = jnp.cumsum(
        decay_blocks.reshape(layout[0], layout[1] * layout[2], layout[3]), axis=1
    ).reshape(layout)
    fading_factor = jnp.exp(cumulative[:, -1, -1, :])
    query_fading = query_blocks * jnp.exp(cumulative)
    return (query_fading, fading_factor, local_out, local_state)


def finish(sequence_segments, incoming_state):
    query_fading, fading_factor, local_out, local_state = sequence_segments
    across_pieces = jnp.einsum(
        "qwxg,qgf->qwxf", query_fading, incoming_state, precision=TOP_PRECISION
    )
    return (
        from_heads(local_out + across_pieces),
        fading_factor[:, :, None] * incoming_state + local_state,
    )


def chain_join(earlier, later):
    return (earlier[0] * later[0], later[0][:, :, None] * earlier[1] + later[1])


def local(
    block_input,
    cotangent,
    attn_gain,
    w_query,
    w_key,
    w_value,
    w_outgate,
    w_decay_down,
    w_decay_up,
    decay_bias,
    head_gain,
    w_out,
    mlp_gain,
    w_gate,
    w_up,
    w_down,
):
    weights = (
        lax.all_gather(attn_gain, "seq", axis=0, tiled=True),
        lax.all_gather(w_query, "seq", axis=0, tiled=True),
        lax.all_gather(w_key, "seq", axis=0, tiled=True),
        lax.all_gather(w_value, "seq", axis=0, tiled=True),
        lax.all_gather(w_outgate, "seq", axis=0, tiled=True),
        lax.all_gather(w_decay_down, "seq", axis=0, tiled=True),
        lax.all_gather(w_decay_up, "seq", axis=1, tiled=True),
        lax.all_gather(decay_bias, "seq", axis=0, tiled=True),
        lax.all_gather(head_gain, "seq", axis=0, tiled=True),
        lax.all_gather(w_out, "seq", axis=0, tiled=True),
        lax.all_gather(mlp_gain, "seq", axis=0, tiled=True),
        lax.all_gather(w_gate, "seq", axis=0, tiled=True),
        lax.all_gather(w_up, "seq", axis=0, tiled=True),
        lax.all_gather(w_down, "seq", axis=0, tiled=True),
    )
    scaling = DK ** (-0.5)
    normed, norm_back = jax.vjp(rms_norm, block_input, weights[0].astype(jnp.float32))
    normed_in = normed.astype(jnp.bfloat16)
    query = matmul(normed_in, weights[1]) * scaling
    keys = matmul(normed_in, weights[2])
    values = matmul(normed_in, weights[3])
    outgate = matmul(normed_in, weights[4])
    low_rank = matmul(normed_in, weights[5]).astype(jnp.bfloat16)
    decay_logit = matmul(low_rank, weights[6]) + weights[7].astype(jnp.float32)
    sequence_segments, local_back = jax.vjp(local_pass, query, keys, values, decay_logit)
    prefix = carried_in(
        (sequence_segments[1], sequence_segments[3]),
        "seq",
        chain_join,
        (jnp.ones_like(sequence_segments[1]), jnp.zeros_like(sequence_segments[3])),
    )
    incoming_state = prefix[1]
    mixer, state_after = finish(sequence_segments, incoming_state)
    gated_full, post_back = jax.vjp(post_gate, mixer, outgate, weights[8].astype(jnp.float32))
    gated = gated_full.astype(jnp.bfloat16)
    hidden_state = block_input + matmul(gated, weights[9])
    mlp_full, mlp_back = jax.vjp(rms_norm, hidden_state, weights[10].astype(jnp.float32))
    mlp_normed = mlp_full.astype(jnp.bfloat16)
    gate_pre = matmul(mlp_normed, weights[11])
    up_pre = matmul(mlp_normed, weights[12])
    activ_full, activ_back = jax.vjp(swiglu, gate_pre, up_pre)
    activ = activ_full.astype(jnp.bfloat16)
    block_output = hidden_state + matmul(activ, weights[13])
    cot_in = cotangent.astype(jnp.bfloat16)
    grad_down = outer_sum(activ, cot_in)
    d_activ = times_back(cot_in, weights[13])
    d_gate_full, d_up_full = activ_back(d_activ)
    d_gate = d_gate_full.astype(jnp.bfloat16)
    d_up = d_up_full.astype(jnp.bfloat16)
    grad_gate = outer_sum(mlp_normed, d_gate)
    grad_up = outer_sum(mlp_normed, d_up)
    d_mlp_normed = times_back(d_gate, weights[11]) + times_back(d_up, weights[12])
    d_hidden_norm, grad_mlp_gain = mlp_back(d_mlp_normed)
    d_hidden = cotangent + d_hidden_norm
    d_hidden_in = d_hidden.astype(jnp.bfloat16)
    grad_out = outer_sum(gated, d_hidden_in)
    d_gated = times_back(d_hidden_in, weights[9])
    mixer_gradient, d_outgate, grad_head_gain = post_back(d_gated)
    state_gradient = jnp.einsum(
        "ryfm,ryfj->rmj",
        sequence_segments[0],
        split_into_heads(mixer_gradient, VALUE_WIDTH),
        precision=TOP_PRECISION,
    )
    suffix = entering(
        (sequence_segments[1], state_gradient),
        "seq",
        chain_join,
        (jnp.ones_like(sequence_segments[1]), jnp.zeros_like(state_gradient)),
    )
    finish_value, finish_back = jax.vjp(finish, sequence_segments, incoming_state)
    d_pieces, d_incoming = finish_back((mixer_gradient, suffix[1]))
    d_query, d_keys, d_values, d_logit = local_back(d_pieces)
    grad_decay_bias = jnp.sum(d_logit, axis=0)
    d_logit_in = d_logit.astype(jnp.bfloat16)
    grad_decay_up = outer_sum(low_rank, d_logit_in)
    d_low = times_back(d_logit_in, weights[6]).astype(jnp.bfloat16)
    grad_decay_down = outer_sum(normed_in, d_low)
    d_query_in = (d_query * scaling).astype(jnp.bfloat16)
    d_keys_in = d_keys.astype(jnp.bfloat16)
    d_values_in = d_values.astype(jnp.bfloat16)
    d_outgate_in = d_outgate.astype(jnp.bfloat16)
    grad_query = outer_sum(normed_in, d_query_in)
    grad_key = outer_sum(normed_in, d_keys_in)
    grad_value = outer_sum(normed_in, d_values_in)
    grad_outgate = outer_sum(normed_in, d_outgate_in)
    d_normed = (
        times_back(d_query_in, weights[1])
        + times_back(d_keys_in, weights[2])
        + times_back(d_values_in, weights[3])
    )
    d_normed = d_normed + times_back(d_outgate_in, weights[4]) + times_back(d_low, weights[5])
    d_input_norm, grad_attn_gain = norm_back(d_normed)
    input_grad = d_hidden + d_input_norm
    summed = (
        lax.psum_scatter(grad_attn_gain, "seq", scatter_dimension=0, tiled=True),
        lax.psum_scatter(grad_query, "seq", scatter_dimension=0, tiled=True),
        lax.psum_scatter(grad_key, "seq", scatter_dimension=0, tiled=True),
        lax.psum_scatter(grad_value, "seq", scatter_dimension=0, tiled=True),
        lax.psum_scatter(grad_outgate, "seq", scatter_dimension=0, tiled=True),
        lax.psum_scatter(grad_decay_down, "seq", scatter_dimension=0, tiled=True),
        lax.psum_scatter(grad_decay_up, "seq", scatter_dimension=1, tiled=True),
        lax.psum_scatter(grad_decay_bias, "seq", scatter_dimension=0, tiled=True),
        lax.psum_scatter(grad_head_gain, "seq", scatter_dimension=0, tiled=True),
        lax.psum_scatter(grad_out, "seq", scatter_dimension=0, tiled=True),
        lax.psum_scatter(grad_mlp_gain, "seq", scatter_dimension=0, tiled=True),
        lax.psum_scatter(grad_gate, "seq", scatter_dimension=0, tiled=True),
        lax.psum_scatter(grad_up, "seq", scatter_dimension=0, tiled=True),
        lax.psum_scatter(grad_down, "seq", scatter_dimension=0, tiled=True),
    )
    return (block_output, input_grad) + tuple(summed)


def solution(mesh):
    return jax.shard_map(
        local,
        mesh=mesh,
        in_specs=(
            P("seq", None),
            P("seq", None),
            P("seq"),
            P("seq", None),
            P("seq", None),
            P("seq", None),
            P("seq", None),
            P("seq", None),
            P(None, "seq"),
            P("seq"),
            P("seq"),
            P("seq", None),
            P("seq"),
            P("seq", None),
            P("seq", None),
            P("seq", None),
        ),
        out_specs=(
            P("seq", None),
            P("seq", None),
            P("seq"),
            P("seq", None),
            P("seq", None),
            P("seq", None),
            P("seq", None),
            P("seq", None),
            P(None, "seq"),
            P("seq"),
            P("seq"),
            P("seq", None),
            P("seq"),
            P("seq", None),
            P("seq", None),
            P("seq", None),
        ),
        check_vma=False,
    )
```

profile of v0, /device:TPU:0, one launch (start us, length us, event | category | flops | bytes accessed | tf_op | source)
XLA Modules:
  0.0 2252.7 jit_solution(7982231192376862782)
XLA Ops:
  12.9 42.1 %all-reduce.11 = (bf16[1024]{0:T(1024)(128)(2,1)S(1)}, bf16[512]{0:T(512)(128)(2,1)S(1)}, bf16[256]{0:T(256)(128)(2,1)}, bf16[1024]{0:T(1024)(128)(2,1)}) all-reduce(bf16[1024]{0:T(1024)(128)(2,1)S(1)} %dynamic-update-slice, bf16[512]{0:T(512)(128)(2,1)S(1)} %dynamic-update-slice.1, ...), channel_id=1, replica_groups=mesh['seq'=32] {'seq'}, use_global_device_ids=true, to_apply=%add.2 | all-reduce | flops 2816 | bytes 11264
  55.0 41.0 %all-gather.4 = bf16[32,32,16]{1,2,0:T(8,128)(2,1)S(1)} all-gather(bf16[1,32,16]{1,2,0:T(8,128)(2,1)} %bitcast.428), channel_id=1, replica_groups=mesh['seq'=32] {'seq'}, dimensions={0}, use_global_device_ids=true | all-gather | bytes 33792 | tf_op jit(solution)/shard_map/all_gather | solution.py:190
  97.0 37.1 %all_gather.65 = bf16[16,512]{0,1:T(8,128)(2,1)S(1)} all-gather(bf16[16,16]{0,1:T(8,128)(2,1)S(1)} %copy.116), channel_id=1, replica_groups=mesh['seq'=32] {'seq'}, dimensions={1}, use_global_device_ids=true | all-gather | bytes 16896 | tf_op jit(solution)/shard_map/all_gather | solution.py:191
  143.4 37.6 %all-gather.20.cloned.1.call-done = bf16[1024,1024]{1,0:T(8,128)(2,1)} async-done(((bf16[32,1024]{1,0:T(8,128)(2,1)}), bf16[1024,1024]{1,0:T(8,128)(2,1)}) %all-gather.20.cloned.1.call-update) | async-done | bytes 2097168 | tf_op jit(solution)/shard_map/all_gather | solution.py:188
  199.9 42.6 %all-gather = f32[128,1,1,128]{3,2,1,0:T(1,128)} all-gather(f32[4,1,1,128]{3,2,1,0:T(1,128)S(1)} %get-tuple-element.779), channel_id=2, replica_groups=mesh['seq'=32] {'seq'}, dimensions={0}, use_global_device_ids=true | all-gather | bytes 67584 | tf_op jit(solution)/shard_map/all_gather | solution.py:19
  245.4 59.3 %all-gather.32.cloned.1.call-done = f32[128,128,256]{2,1,0:T(8,128)} async-done(((f32[4,128,256]{2,1,0:T(8,128)}), f32[128,128,256]{2,1,0:T(8,128)}) %all-gather.32.cloned.1.call-update) | async-done | bytes 16777232 | tf_op jit(solution)/shard_map/all_gather | solution.py:19
  304.7 59.5 %while.71 = (s32[]{:T(128)}, f32[4,128,256]{2,1,0:T(8,128)S(1)}, s32[]{:T(128)}, f32[32,4,128]{2,1,0:T(4,128)}, f32[32,4,128,256]{3,2,1,0:T(8,128)}, /*index=5*/s32[]{:T(128)}, s32[]{:T(128)}) while((s32[]{:T(128)}, f32[4,128,256]{2,1,0:T(8,128)S(1)}, s32[]{:T(128)}, f32[32,4,128]{2,1,0:T(4,128)}, f32[32,4,128,256]{3,2,1,0:T(8,128)}, ...), condition=%wide.region_6.7_spmd.clone, body=%wide.region_5.6_spmd.clone.sunk | while | flops 524292 | bytes 1579121 | solution.py:28
  372.8 46.9 %all-gather.24.cloned.1.call-done = bf16[1024,1024]{1,0:T(8,128)(2,1)} async-done(((bf16[32,1024]{1,0:T(8,128)(2,1)}), bf16[1024,1024]{1,0:T(8,128)(2,1)}) %all-gather.24.cloned.1.call-update) | async-done | bytes 2097168 | tf_op jit(solution)/shard_map/all_gather | solution.py:194
  422.5 66.2 %all-gather.26.cloned.1.call-done = bf16[1024,2816]{1,0:T(8,128)(2,1)} async-done(((bf16[32,2816]{1,0:T(8,128)(2,1)}), bf16[1024,2816]{1,0:T(8,128)(2,1)}) %all-gather.26.cloned.1.call-update) | async-done | bytes 5767184 | tf_op jit(solution)/shard_map/all_gather | solution.py:196
  493.4 64.1 %all-gather.28.cloned.1.call-done = bf16[1024,2816]{1,0:T(8,128)(2,1)} async-done(((bf16[32,2816]{1,0:T(8,128)(2,1)}), bf16[1024,2816]{1,0:T(8,128)(2,1)}) %all-gather.28.cloned.1.call-update) | async-done | bytes 5767184 | tf_op jit(solution)/shard_map/all_gather | solution.py:197
  562.2 64.2 %all-gather.30.cloned.1.call-done = bf16[2816,1024]{1,0:T(8,128)(2,1)} async-done(((bf16[88,1024]{1,0:T(8,128)(2,1)}), bf16[2816,1024]{1,0:T(8,128)(2,1)}) %all-gather.30.cloned.1.call-update) | async-done | bytes 5767184 | tf_op jit(solution)/shard_map/all_gather | solution.py:198
  652.0 40.0 %all-gather.3 = bf16[128,1,1,128]{3,2,1,0:T(2,128)(2,1)S(1)} all-gather(bf16[4,1,1,128]{3,2,1,0:T(2,128)(2,1)S(1)} %copy-done.67), channel_id=5, replica_groups=mesh['seq'=32] {'seq'}, dimensions={0}, use_global_device_ids=true | all-gather | bytes 33792 | tf_op jit(solution)/shard_map/all_gather | solution.py:34
  727.4 59.3 %while.72 = (s32[]{:T(128)}, f32[4,128,256]{2,1,0:T(8,128)S(1)}, s32[]{:T(128)}, bf16[32,4,128]{2,1,0:T(4,128)(2,1)}, bf16[32,4,128,256]{3,2,1,0:T(8,128)(2,1)},...) while((s32[]{:T(128)}, f32[4,128,256]{2,1,0:T(8,128)S(1)}, s32[]{:T(128)}, ...), condition=%wide.region_12.13_spmd.clone, body=%wide.region_11.12_spmd.clone.sunk | while | flops 655880 | bytes 1316015 | solution.py:52
  861.5 39.5 %all-reduce.10 = (f32[1024]{0:T(1024)S(1)}, f32[512]{0:T(512)S(1)}, f32[256]{0:T(256)S(1)}, f32[1024]{0:T(1024)S(1)}) all-reduce(f32[1024]{0:T(1024)S(1)} %get-tuple-element.693, f32[512]{0:T(512)S(1)} %neg.61, f32[256]{0:T(256)S(1)} %copy-done.72, f32[1024]{0:T(1024)S(1)} %copy-done.60), channel_id=6, replica_groups=mesh['seq'=32] {'seq'}, use_global_device_ids=true, to_apply=%region_22.23.clone | all-reduce | flops 2816 | bytes 22528
  904.3 44.1 %reduce-scatter.33.cloned.1.call-done = f32[16,16]{1,0:T(8,128)} async-done(((f32[512,16]{1,0:T(8,128)}), f32[16,16]{1,0:T(8,128)}) %reduce-scatter.33.cloned.1.call-update) | async-done | bytes 1040
  949.8 132.4 %reduce-scatter.31.cloned.1.call-done = f32[32,16]{1,0:T(8,128)} async-done(((f32[1024,16]{1,0:T(8,128)}), f32[32,16]{1,0:T(8,128)}) %reduce-scatter.31.cloned.1.call-update) | async-done | bytes 2064
  1083.6 140.0 %reduce-scatter.21.cloned.1.call-done = f32[32,1024]{1,0:T(8,128)} async-done(((f32[1024,1024]{1,0:T(8,128)}), f32[32,1024]{1,0:T(8,128)}) %reduce-scatter.21.cloned.1.call-update) | async-done | bytes 131088 | tf_op jit(solution)/shard_map/reduce_scatter | solution.py:284
  1223.5 141.3 %reduce-scatter.23.cloned.1.call-done = f32[32,1024]{1,0:T(8,128)} async-done(((f32[1024,1024]{1,0:T(8,128)}), f32[32,1024]{1,0:T(8,128)}) %reduce-scatter.23.cloned.1.call-update) | async-done | bytes 131088 | tf_op jit(solution)/shard_map/reduce_scatter | solution.py:289
  1364.8 137.0 %reduce-scatter.15.cloned.1.call-done = f32[32,512]{1,0:T(8,128)} async-done(((f32[1024,512]{1,0:T(8,128)}), f32[32,512]{1,0:T(8,128)}) %reduce-scatter.15.cloned.1.call-update) | async-done | bytes 65552 | tf_op jit(solution)/shard_map/reduce_scatter | solution.py:281
  1501.8 137.1 %reduce-scatter.17.cloned.1.call-done = f32[32,512]{1,0:T(8,128)} async-done(((f32[1024,512]{1,0:T(8,128)}), f32[32,512]{1,0:T(8,128)}) %reduce-scatter.17.cloned.1.call-update) | async-done | bytes 65552 | tf_op jit(solution)/shard_map/reduce_scatter | solution.py:282
  1638.9 155.1 %reduce-scatter.25.cloned.1.call-done = f32[32,2816]{1,0:T(8,128)} async-done(((f32[1024,2816]{1,0:T(8,128)}), f32[32,2816]{1,0:T(8,128)}) %reduce-scatter.25.cloned.1.call-update) | async-done | bytes 360464 | tf_op jit(solution)/shard_map/reduce_scatter | solution.py:291
  1794.0 154.9 %reduce-scatter.27.cloned.1.call-done = f32[32,2816]{1,0:T(8,128)} async-done(((f32[1024,2816]{1,0:T(8,128)}), f32[32,2816]{1,0:T(8,128)}) %reduce-scatter.27.cloned.1.call-update) | async-done | bytes 360464 | tf_op jit(solution)/shard_map/reduce_scatter | solution.py:292
  1948.9 155.3 %reduce-scatter.29.cloned.1.call-done = f32[88,1024]{1,0:T(8,128)} async-done(((f32[2816,1024]{1,0:T(8,128)}), f32[88,1024]{1,0:T(8,128)}) %reduce-scatter.29.cloned.1.call-update) | async-done | bytes 360464 | tf_op jit(solution)/shard_map/reduce_scatter | solution.py:293
  2104.2 141.5 %reduce-scatter.19.cloned.1.call-done = f32[32,1024]{1,0:T(8,128)} async-done(((f32[1024,1024]{1,0:T(8,128)}), f32[32,1024]{1,0:T(8,128)}) %reduce-scatter.19.cloned.1.call-update) | async-done | bytes 131088 | tf_op jit(solution)/shard_map/reduce_scatter | solution.py:283
  (478 shorter events, 331.4 us)
Async XLA Ops:
  7.2 132.0 %all-gather.16.cloned.1.call-start = ((), (), s32[]{:S(2)}) async-start(), calls=%async_computation.10 | async-start | bytes 1081344 | tf_op jit(solution)/shard_map/all_gather | solution.py:186
  7.9 133.0 %all-gather.18.cloned.1.call-start = ((), (), s32[]{:S(2)}) async-start(), calls=%async_computation.11 | async-start | bytes 1081344 | tf_op jit(solution)/shard_map/all_gather | solution.py:187
  8.7 172.4 %all-gather.20.cloned.1.call-start = ((), (), s32[]{:S(2)}) async-start(), calls=%async_computation.12 | async-start | bytes 2162688 | tf_op jit(solution)/shard_map/all_gather | solution.py:188
  9.4 295.3 %all-gather.32.cloned.1.call-start = ((), (), s32[]{:S(2)}) async-start(), calls=%async_computation.26 | async-start | bytes 17301504 | tf_op jit(solution)/shard_map/all_gather | solution.py:19
  140.9 223.3 %copy-start.8 = (f32[2,64,4,128]{3,2,1,0:T(4,128)}, f32[2,64,4,128]{3,2,1,0:T(4,128)S(1)}, u32[]{:S(2)}) copy-start(f32[2,64,4,128]{3,2,1,0:T(4,128)S(1)} %reshape.213) | copy-start | bytes 786436
  189.9 114.8 %copy-start.13 = (f32[2,4,64,128]{3,2,1,0:T(8,128)}, f32[2,4,64,128]{3,2,1,0:T(8,128)S(1)}, u32[]{:S(2)}) copy-start(f32[2,4,64,128]{3,2,1,0:T(8,128)S(1)} %get-tuple-element.1145) | copy-start | bytes 786436
  190.8 178.6 %all-gather.22.cloned.1.call-start = ((), (), s32[]{:S(2)}) async-start(), calls=%async_computation.13 | async-start | bytes 2162688 | tf_op jit(solution)/shard_map/all_gather | solution.py:189
  191.3 228.3 %all-gather.24.cloned.1.call-start = ((), (), s32[]{:S(2)}) async-start(), calls=%async_computation.14 | async-start | bytes 2162688 | tf_op jit(solution)/shard_map/all_gather | solution.py:194
  191.9 296.8 %all-gather.26.cloned.1.call-start = ((), (), s32[]{:S(2)}) async-start(), calls=%async_computation.15 | async-start | bytes 5947392 | tf_op jit(solution)/shard_map/all_gather | solution.py:196
  192.7 364.9 %all-gather.28.cloned.1.call-start = ((), (), s32[]{:S(2)}) async-start(), calls=%async_computation.16 | async-start | bytes 5947392 | tf_op jit(solution)/shard_map/all_gather | solution.py:197
  193.4 433.0 %all-gather.30.cloned.1.call-start = ((), (), s32[]{:S(2)}) async-start(), calls=%async_computation.17 | async-start | bytes 5947392 | tf_op jit(solution)/shard_map/all_gather | solution.py:198
  194.2 533.3 %all-gather.34.cloned.1.call-start = ((), (), s32[]{:S(2)}) async-start(), calls=%async_computation.27 | async-start | bytes 8650752 | tf_op jit(solution)/shard_map/all_gather | solution.py:34
  421.9 219.2 %copy-start.2 = (f32[128,1024]{1,0:T(8,128)}, f32[128,1024]{1,0:T(8,128)S(1)}, u32[]{:S(2)}) copy-start(f32[128,1024]{1,0:T(8,128)S(1)} %get-tuple-element.792) | copy-start | bytes 1572868
  422.5 135.0 %copy-start.11 = (bf16[128,1024]{1,0:T(8,128)(2,1)}, bf16[128,1024]{1,0:T(8,128)(2,1)S(1)}, u32[]{:S(2)}) copy-start(bf16[128,1024]{1,0:T(8,128)(2,1)S(1)} %multiply_convert_fusion.2) | copy-start | bytes 786436
  651.5 296.9 %reduce-scatter.33.cloned.1.call-start = ((), (), s32[]{:S(2)}) async-start(), calls=%async_computation.29 | async-start | bytes 270336
  814.0 268.2 %reduce-scatter.31.cloned.1.call-start = ((), (), s32[]{:S(2)}) async-start(), calls=%async_computation.28 | async-start | bytes 540672
  815.3 408.2 %reduce-scatter.21.cloned.1.call-start = ((), (), s32[]{:S(2)}) async-start(), calls=%async_computation.21 | async-start | bytes 4325376 | tf_op jit(solution)/shard_map/reduce_scatter | solution.py:284
  818.0 546.8 %reduce-scatter.23.cloned.1.call-start = ((), (), s32[]{:S(2)}) async-start(), calls=%async_computation.22 | async-start | bytes 4325376 | tf_op jit(solution)/shard_map/reduce_scatter | solution.py:289
  821.8 680.0 %reduce-scatter.15.cloned.1.call-start = ((), (), s32[]{:S(2)}) async-start(), calls=%async_computation.18 | async-start | bytes 2162688 | tf_op jit(solution)/shard_map/reduce_scatter | solution.py:281
  823.8 815.0 %reduce-scatter.17.cloned.1.call-start = ((), (), s32[]{:S(2)}) async-start(), calls=%async_computation.19 | async-start | bytes 2162688 | tf_op jit(solution)/shard_map/reduce_scatter | solution.py:282
  825.8 968.2 %reduce-scatter.25.cloned.1.call-start = ((), (), s32[]{:S(2)}) async-start(), calls=%async_computation.23 | async-start | bytes 11894784 | tf_op jit(solution)/shard_map/reduce_scatter | solution.py:291
  831.8 1117.1 %reduce-scatter.27.cloned.1.call-start = ((), (), s32[]{:S(2)}) async-start(), calls=%async_computation.24 | async-start | bytes 11894784 | tf_op jit(solution)/shard_map/reduce_scatter | solution.py:292
  838.8 1265.4 %reduce-scatter.29.cloned.1.call-start = ((), (), s32[]{:S(2)}) async-start(), calls=%async_computation.25 | async-start | bytes 11894784 | tf_op jit(solution)/shard_map/reduce_scatter | solution.py:293
  845.9 1399.8 %reduce-scatter.19.cloned.1.call-start = ((), (), s32[]{:S(2)}) async-start(), calls=%async_computation.20 | async-start | bytes 4325376 | tf_op jit(solution)/shard_map/reduce_scatter | solution.py:283
  (76 other events, 742.8 us)
Sparse Core Ops, SparseCore 0:
  10.8 56.4 all-gather.15
  70.2 52.6 all-gather.17
  125.7 55.2 all-gather.19
  190.9 113.7 all-gather.31
  307.4 54.4 all-gather.21
  364.6 55.0 all-gather.23
  422.5 66.1 all-gather.25
  491.5 65.9 all-gather.27
  560.4 65.9 all-gather.29
  651.6 75.7 all-gather.33
  814.1 134.2 reduce-scatter.32
  950.5 131.6 reduce-scatter.30
  1085.0 138.4 reduce-scatter.20
  1226.2 138.5 reduce-scatter.22
  1367.5 134.2 reduce-scatter.14
  1504.5 134.3 reduce-scatter.16
  1641.6 152.3 reduce-scatter.24
  1796.7 152.1 reduce-scatter.26
  1951.8 152.3 reduce-scatter.28
  2106.9 138.7 reduce-scatter.18
where the time goes:
time: 2260 us; the launch traced here: 2250 us
  waiting for transfers between devices  1710 us (76%)
  blocking collectives  242 us (11%)
  other arithmetic  119 us (5%)
  matrix products  105 us (5%)
  local copies, waits for them, and re-layouts  54.5 us (2%)
    unnamed x22, waiting for transfers between devices  182 us
    reduce_scatter x1, waiting for transfers between devices, local(): lax.psum_scatter(grad_down, 'seq', scatter_dimension=0, tiled=True)  155 us
    reduce_scatter x1, waiting for transfers between devices, local(): lax.psum_scatter(grad_gate, 'seq', scatter_dimension=0, tiled=True)  155 us
    reduce_scatter x1, waiting for transfers between devices, local(): lax.psum_scatter(grad_up, 'seq', scatter_dimension=0, tiled=True)  155 us
    reduce_scatter x1, waiting for transfers between devices, local(): lax.psum_scatter(grad_value, 'seq', scatter_dimension=0, tiled=True)  141 us
    reduce_scatter x1, waiting for transfers between devices, local(): lax.psum_scatter(grad_out, 'seq', scatter_dimension=0, tiled=True)  141 us
    reduce_scatter x1, waiting for transfers between devices, local(): lax.psum_scatter(grad_outgate, 'seq', scatter_dimension=0, tiled=True)  140 us
    reduce_scatter x1, waiting for transfers between devices, local(): lax.psum_scatter(grad_key, 'seq', scatter_dimension=0, tiled=True)  137 us
  transfers between devices with their start and end apart: 20, of which 17 were waited for; matrix products, arithmetic and copies ran while one was open for 7% of the time, Pallas kernels for 0%

commit v1 on v0

v1 whole, which is shorter than its diff:
```python
import jax
import jax.numpy as jnp
from jax import lax
from jax.sharding import PartitionSpec as P

H = 4
DK = 128
VALUE_WIDTH = 256
GROUP = 64


EPS = 1e-05
GATE_NORM = 16.0
TOP_PRECISION = lax.Precision.HIGHEST


LANES = 128


def pack_small(pieces, rows):
    flat = jnp.concatenate([piece.reshape(-1) for piece in pieces])
    return jnp.pad(flat, (0, rows * LANES - flat.shape[0])).reshape(rows, LANES)


def pack_small_sums(pieces, devices, rows):
    flat = jnp.concatenate([piece.reshape(devices, -1) for piece in pieces], axis=1)
    flat = jnp.pad(flat, ((0, 0), (0, rows * LANES - flat.shape[1])))
    return flat.reshape(devices * rows, LANES)


def unpack_small(flat, shapes):
    pieces, at = [], 0
    for shape in shapes:
        size = 1
        for extent in shape:
            size *= extent
        pieces.append(flat[..., at : at + size].reshape(flat.shape[:-1] + shape))
        at += size
    return pieces


def column_slices(array, widths):
    pieces, at = [], 0
    for width in widths:
        pieces.append(array[:, at : at + width])
        at += width
    return pieces


def three_pieces(value):
    high = value.astype(jnp.bfloat16)
    rest = value - high.astype(jnp.float32)
    middle = rest.astype(jnp.bfloat16)
    low = (rest - middle.astype(jnp.float32)).astype(jnp.bfloat16)
    return jnp.stack([high, middle, low])


def between(log_fading, mine, forward):
    count = log_fading.shape[0]
    j = lax.broadcasted_iota(jnp.int32, (count, count), 0)
    k = lax.broadcasted_iota(jnp.int32, (count, count), 1)
    if forward:
        inside = (j < k) & (k < mine)
        taken = jnp.arange(count) < mine
    else:
        inside = (k < j) & (k > mine)
        taken = jnp.arange(count) > mine
    span = jnp.dot(inside.astype(jnp.float32), log_fading, precision=TOP_PRECISION)
    return jnp.where(taken[:, None], jnp.exp(span), 0.0)


def matmul(left_side, right_side):
    return jnp.dot(left_side, right_side, preferred_element_type=jnp.float32)


def times_back(left_side, right_side):
    return lax.dot_general(
        left_side, right_side, (((1,), (1,)), ((), ())), preferred_element_type=jnp.float32
    )


def outer_sum(left_side, right_side):
    return lax.dot_general(
        left_side, right_side, (((0,), (0,)), ((), ())), preferred_element_type=jnp.float32
    )


def rms_norm(matrix, gain):
    scaling = lax.rsqrt(jnp.mean(matrix * matrix, axis=-1, keepdims=True) + EPS)
    return matrix * scaling * gain


def swiglu(gate_pre, up_pre):
    return jax.nn.silu(gate_pre) * up_pre


def split_into_heads(matrix, columns):
    return matrix.reshape(matrix.shape[0] // GROUP, GROUP, H, columns).transpose(2, 0, 1, 3)


def from_heads(blocks):
    return blocks.transpose(1, 2, 0, 3).reshape(
        blocks.shape[1] * blocks.shape[2], blocks.shape[0] * blocks.shape[3]
    )


def to_front(tensor):
    return jnp.moveaxis(tensor, 1, 0)


def group_pass(query_blocks, key_blocks, value_blocks, decay_blocks, initial):
    inner = jnp.cumsum(decay_blocks, axis=2)
    ending = inner[:, :, -1:, :]
    query_in = query_blocks * jnp.exp(inner)
    key_in = key_blocks * jnp.exp(-inner)
    key_end = key_blocks * jnp.exp(ending - inner)
    length = query_blocks.shape[2]
    causal = jnp.tril(jnp.ones((length, length), jnp.float32))
    scores = jnp.einsum("hnck,hnsk->hncs", query_in, key_in, precision=TOP_PRECISION) * causal
    within = jnp.einsum("hncs,hnsv->hncv", scores, value_blocks, precision=TOP_PRECISION)

    def advance(carried_state, sequence_segments):
        query_segment, key_segment, value_segment, fading_factor = sequence_segments
        block_result = jnp.einsum(
            "waq,wqo->wao", query_segment, carried_state, precision=TOP_PRECISION
        )
        carried_state = fading_factor[:, 0, :, None] * carried_state + jnp.einsum(
            "fjb,fjq->fbq", key_segment, value_segment, precision=TOP_PRECISION
        )
        return (carried_state, block_result)

    final, across_pieces = lax.scan(
        advance,
        initial,
        (to_front(query_in), to_front(key_end), to_front(value_blocks), to_front(jnp.exp(ending))),
    )
    return (within + to_front(across_pieces), final)


def post_gate(mixer, outgate, head_gain):
    tokens_here = mixer.shape[0]
    per_head = mixer.reshape(tokens_here, H, VALUE_WIDTH)
    normed = rms_norm(per_head, head_gain).reshape(tokens_here, H * VALUE_WIDTH)
    return normed * outgate * jax.nn.sigmoid(outgate)


def local_pass(query, keys, values, decay_logit):
    log_decay = jax.nn.log_sigmoid(decay_logit) / GATE_NORM
    query_blocks = split_into_heads(query, DK)
    decay_blocks = split_into_heads(log_decay, DK)
    zero_state = jnp.zeros((H, DK, VALUE_WIDTH), jnp.float32)
    local_out, local_state = group_pass(
        query_blocks,
        split_into_heads(keys, DK),
        split_into_heads(values, VALUE_WIDTH),
        decay_blocks,
        zero_state,
    )
    layout = decay_blocks.shape
    cumulative = jnp.cumsum(
        decay_blocks.reshape(layout[0], layout[1] * layout[2], layout[3]), axis=1
    ).reshape(layout)
    log_fading = cumulative[:, -1, -1, :]
    query_fading = query_blocks * jnp.exp(cumulative)
    return (query_fading, log_fading, local_out, local_state)


def finish(sequence_segments, incoming_state):
    query_fading, log_fading, local_out, local_state = sequence_segments
    across_pieces = jnp.einsum(
        "qwxg,qgf->qwxf", query_fading, incoming_state, precision=TOP_PRECISION
    )
    return (
        from_heads(local_out + across_pieces),
        jnp.exp(log_fading)[:, :, None] * incoming_state + local_state,
    )


def local(
    block_input,
    cotangent,
    attn_gain,
    w_query,
    w_key,
    w_value,
    w_outgate,
    w_decay_down,
    w_decay_up,
    decay_bias,
    head_gain,
    w_out,
    mlp_gain,
    w_gate,
    w_up,
    w_down,
):
    count, mine = (lax.axis_size("seq"), lax.axis_index("seq"))
    rows = w_query.shape[0]
    key_width, value_width, rank = (w_query.shape[1], w_value.shape[1], w_decay_down.shape[1])
    hidden = w_gate.shape[1]
    small_shapes = (w_decay_up.shape, attn_gain.shape, mlp_gain.shape, decay_bias.shape, head_gain.shape)
    first = jnp.concatenate(
        [
            w_query,
            w_key,
            w_value,
            w_outgate,
            jnp.pad(w_decay_down, ((0, 0), (0, LANES - rank))),
            pack_small((w_decay_up, attn_gain, mlp_gain, decay_bias, head_gain), rows),
        ],
        axis=1,
    )
    first = lax.all_gather(first, "seq", axis=0, tiled=True)
    second = jnp.concatenate([w_out, w_gate, w_up], axis=1)
    second = lax.all_gather(second, "seq", axis=0, tiled=True)
    down_full = lax.all_gather(w_down, "seq", axis=0, tiled=True)
    widths = (key_width, key_width, value_width, value_width)
    wide = 2 * key_width + 2 * value_width
    projection = first[:, : wide + LANES]
    small = first[:, wide + LANES :].reshape(count, rows * LANES)
    up_pieces, attn_full, mlp_full_gain, bias_full, head_full = unpack_small(small, small_shapes)
    decay_up_full = up_pieces.transpose(1, 0, 2).reshape(rank, key_width)
    attn_full, mlp_full_gain, bias_full, head_full = (
        piece.reshape(-1).astype(jnp.float32) for piece in (attn_full, mlp_full_gain, bias_full, head_full)
    )
    out_full = second[:, : w_out.shape[1]]
    gate_up = second[:, w_out.shape[1] :]
    scaling = DK ** (-0.5)
    normed, norm_back = jax.vjp(rms_norm, block_input, attn_full)
    normed_in = normed.astype(jnp.bfloat16)
    query, keys, values, outgate, low_rank = column_slices(
        matmul(normed_in, projection), widths + (rank,)
    )
    query = query * scaling
    low_rank = low_rank.astype(jnp.bfloat16)
    decay_logit = matmul(low_rank, decay_up_full) + bias_full
    sequence_segments, local_back = jax.vjp(local_pass, query, keys, values, decay_logit)
    state = sequence_segments[3].reshape(key_width, VALUE_WIDTH).astype(jnp.bfloat16)
    log_rows = three_pieces(sequence_segments[1].reshape(-1)).reshape(-1, VALUE_WIDTH)
    extra = log_rows.shape[0]
    log_rows = jnp.pad(log_rows, ((0, -extra % 16), (0, 0)))
    everything = lax.all_gather(jnp.concatenate([state, log_rows], axis=0), "seq")
    log_fading = everything[:, key_width : key_width + extra].astype(jnp.float32)
    log_fading = log_fading.reshape(count, 3, key_width).sum(axis=1)
    weight = between(log_fading, mine, True)
    incoming_state = jnp.sum(
        weight[:, :, None] * everything[:, :key_width].astype(jnp.float32), axis=0
    ).reshape(H, DK, VALUE_WIDTH)
    mixer, state_after = finish(sequence_segments, incoming_state)
    gated_full, post_back = jax.vjp(post_gate, mixer, outgate, head_full)
    gated = gated_full.astype(jnp.bfloat16)
    hidden_state = block_input + matmul(gated, out_full)
    mlp_full, mlp_back = jax.vjp(rms_norm, hidden_state, mlp_full_gain)
    mlp_normed = mlp_full.astype(jnp.bfloat16)
    gate_pre, up_pre = column_slices(matmul(mlp_normed, gate_up), (hidden, hidden))
    activ_full, activ_back = jax.vjp(swiglu, gate_pre, up_pre)
    activ = activ_full.astype(jnp.bfloat16)
    block_output = hidden_state + matmul(activ, down_full)
    cot_in = cotangent.astype(jnp.bfloat16)
    grad_down = outer_sum(activ, cot_in)
    d_activ = times_back(cot_in, down_full)
    d_gate_full, d_up_full = activ_back(d_activ)
    d_gate = d_gate_full.astype(jnp.bfloat16)
    d_up = d_up_full.astype(jnp.bfloat16)
    d_gate_up = jnp.concatenate([d_gate, d_up], axis=1)
    grad_gate_up = outer_sum(mlp_normed, d_gate_up)
    d_mlp_normed = times_back(d_gate_up, gate_up)
    d_hidden_norm, grad_mlp_gain = mlp_back(d_mlp_normed)
    d_hidden = cotangent + d_hidden_norm
    d_hidden_in = d_hidden.astype(jnp.bfloat16)
    grad_out = outer_sum(gated, d_hidden_in)
    d_gated = times_back(d_hidden_in, out_full)
    mixer_gradient, d_outgate, grad_head_gain = post_back(d_gated)
    state_gradient = jnp.einsum(
        "ryfm,ryfj->rmj",
        sequence_segments[0],
        split_into_heads(mixer_gradient, VALUE_WIDTH),
        precision=TOP_PRECISION,
    )
    everything_back = lax.all_gather(
        state_gradient.reshape(key_width, VALUE_WIDTH).astype(jnp.bfloat16), "seq"
    )
    weight_back = between(log_fading, mine, False)
    after = jnp.sum(weight_back[:, :, None] * everything_back.astype(jnp.float32), axis=0)
    after = after.reshape(H, DK, VALUE_WIDTH)
    finish_value, finish_back = jax.vjp(finish, sequence_segments, incoming_state)
    d_pieces, d_incoming = finish_back((mixer_gradient, after))
    d_query, d_keys, d_values, d_logit = local_back(d_pieces)
    grad_decay_bias = jnp.sum(d_logit, axis=0)
    d_logit_in = d_logit.astype(jnp.bfloat16)
    grad_decay_up = outer_sum(low_rank, d_logit_in)
    d_low = times_back(d_logit_in, decay_up_full).astype(jnp.bfloat16)
    d_first = jnp.concatenate(
        [
            (d_query * scaling).astype(jnp.bfloat16),
            d_keys.astype(jnp.bfloat16),
            d_values.astype(jnp.bfloat16),
            d_outgate.astype(jnp.bfloat16),
            jnp.pad(d_low, ((0, 0), (0, LANES - rank))),
        ],
        axis=1,
    )
    grad_first = outer_sum(normed_in, d_first)
    d_normed = times_back(d_first, projection)
    d_input_norm, grad_attn_gain = norm_back(d_normed)
    input_grad = d_hidden + d_input_norm

    def scattered(partial):
        return lax.psum_scatter(
            partial.astype(jnp.bfloat16), "seq", scatter_dimension=0, tiled=True
        ).astype(jnp.float32)

    sum_down = scattered(grad_down)
    sum_second = scattered(jnp.concatenate([grad_out, grad_gate_up], axis=1))
    small_sums = pack_small_sums(
        (
            grad_decay_up.reshape(rank, count, -1).transpose(1, 0, 2),
            grad_attn_gain,
            grad_mlp_gain,
            grad_decay_bias,
            grad_head_gain,
        ),
        count,
        rows,
    )
    sum_first = scattered(jnp.concatenate([grad_first, small_sums], axis=1))
    sum_query, sum_key, sum_value, sum_outgate, sum_decay_down = column_slices(
        sum_first, widths + (rank,)
    )
    sum_up, sum_attn, sum_mlp, sum_bias, sum_head = unpack_small(
        sum_first[:, wide + LANES :].reshape(-1), small_shapes
    )
    sum_out, sum_gate, sum_up_proj = column_slices(sum_second, (w_out.shape[1], hidden, hidden))
    return (
        block_output,
        input_grad,
        sum_attn,
        sum_query,
        sum_key,
        sum_value,
        sum_outgate,
        sum_decay_down,
        sum_up,
        sum_bias,
        sum_head,
        sum_out,
        sum_mlp,
        sum_gate,
        sum_up_proj,
        sum_down,
    )


def solution(mesh):
    return jax.shard_map(
        local,
        mesh=mesh,
        in_specs=(
            P("seq", None),
            P("seq", None),
            P("seq"),
            P("seq", None),
            P("seq", None),
            P("seq", None),
            P("seq", None),
            P("seq", None),
            P(None, "seq"),
            P("seq"),
            P("seq"),
            P("seq", None),
            P("seq"),
            P("seq", None),
            P("seq", None),
            P("seq", None),
        ),
        out_specs=(
            P("seq", None),
            P("seq", None),
            P("seq"),
            P("seq", None),
            P("seq", None),
            P("seq", None),
            P("seq", None),
            P("seq", None),
            P(None, "seq"),
            P("seq"),
            P("seq"),
            P("seq", None),
            P("seq"),
            P("seq", None),
            P("seq", None),
            P("seq", None),
        ),
        check_vma=False,
    )
```

time: 2260 us -> 929 us (0.41)
  waiting for transfers between devices: 1710 us -> 720 us
  blocking collectives: 242 us -> 0 us
  other arithmetic: 119 us -> 50.9 us
    reduce_scatter x8 -> x3, waiting for transfers between devices: 1160 us -> 387 us  [scattered(): lax.psum_scatter(partial.astype(jnp.bfloat16), 'seq', scatter_dimension=0...]
    unnamed x22 -> x8, waiting for transfers between devices: 182 us -> 0.64 us
    all_gather x4 -> x0, blocking collectives: 161 us -> none  [the longest x1 42.6 us: carried_in(): pieces = jax.tree.map(lambda part: lax.all_gather(part, axis), value)]
    unnamed x2 -> x0, blocking collectives: 81.6 us -> none
    select_n x63 -> x0, other arithmetic: 74.9 us -> none  [the longest x31 38.4 us: carried_hop(): jnp.where(position < mine, new, old)]
    all_gather x10 -> x5, waiting for transfers between devices: 369 us -> 333 us  [the longest x1 84.7 us: local(): second = lax.all_gather(second, 'seq', axis=0, tiled=True)]
  transfers between devices with their start and end apart: 20 -> 8, of which waited for: 17 -> 8; matrix products, arithmetic and copies ran while one was open for 7% -> 13% of each run, Pallas kernels for 0% -> 0%
where the time goes in v1:
time: 929 us; the launch traced here: 923 us
  waiting for transfers between devices  720 us (78%)
  matrix products  89.8 us (10%)
  other arithmetic  50.9 us (5%)
  local copies, waits for them, and re-layouts  45.5 us (5%)
  between operations  15.5 us (2%)
    reduce_scatter x3, waiting for transfers between devices, scattered(): lax.psum_scatter(partial.astype(jnp.bfloat16), 'seq', scatter_dimension=0...  387 us
    all_gather x1, waiting for transfers between devices, local(): second = lax.all_gather(second, 'seq', axis=0, tiled=True)  84.7 us
    all_gather x1, waiting for transfers between devices, local(): first = lax.all_gather(first, 'seq', axis=0, tiled=True)  72.6 us
    all_gather x1, waiting for transfers between devices, local(): lax.all_gather(jnp.concatenate([state, log_rows], axis=0), 'seq')  71.8 us
    all_gather x1, waiting for transfers between devices, local(): down_full = lax.all_gather(w_down, 'seq', axis=0, tiled=True)  58.5 us
    all_gather x1, waiting for transfers between devices, local(): lax.all_gather(state_gradient.reshape(key_width, VALUE_WIDTH).astype(jnp....  45.1 us
    dot_general x5, matrix products, times_back(): lax.dot_general(left_side, right_side, (((1,), (1,)), ((), ())), preferre...  25 us
    dot_general x5, matrix products, matmul(): return jnp.dot(left_side, right_side, preferred_element_type=jnp.float32)  19.5 us
  transfers between devices with their start and end apart: 8, of which 8 were waited for; matrix products, arithmetic and copies ran while one was open for 13% of the time, Pallas kernels for 0%

profile of v1, /device:TPU:0, one launch (start us, length us, event | category | flops | bytes accessed | tf_op | source)
XLA Modules:
  0.0 923.1 jit_solution(5759646371268621326)
XLA Ops:
  16.8 72.6 %all-gather.7.cloned.1.call-done = bf16[1024,3328]{1,0:T(8,128)(2,1)} async-done(((bf16[32,3328]{1,0:T(8,128)(2,1)}), bf16[1024,3328]{1,0:T(8,128)(2,1)}) %all-gather.7.cloned.1.call-update) | async-done | bytes 6815760 | tf_op jit(solution)/shard_map/all_gather | solution.py:213
  91.2 4.2 fusion.40
  103.4 3.8 while.40
  113.0 71.8 %all-gather.15.cloned.1.call-done = bf16[16896,256]{1,0:T(8,128)(2,1)} async-done(((bf16[528,256]{1,0:T(8,128)(2,1)}), bf16[16896,256]{1,0:T(8,128)(2,1)}) %all-gather.15.cloned.1.call-update) | async-done | bytes 8650768 | tf_op jit(solution)/shard_map/all_gather | solution.py:242
  189.6 5.3 multiply_reduce_fusion.1
  201.6 84.7 %all-gather.9.cloned.1.call-done = bf16[1024,6656]{1,0:T(8,128)(2,1)} async-done(((bf16[32,6656]{1,0:T(8,128)(2,1)}), bf16[1024,6656]{1,0:T(8,128)(2,1)}) %all-gather.9.cloned.1.call-update) | async-done | bytes 13631504 | tf_op jit(solution)/shard_map/all_gather | solution.py:215
  288.6 7.8 fusion.36
  296.4 58.5 %all-gather.11.cloned.1.call-done = bf16[2816,1024]{1,0:T(8,128)(2,1)} async-done(((bf16[88,1024]{1,0:T(8,128)(2,1)}), bf16[2816,1024]{1,0:T(8,128)(2,1)}) %all-gather.11.cloned.1.call-update) | async-done | bytes 5767184 | tf_op jit(solution)/shard_map/all_gather | solution.py:216
  354.9 6.8 fusion.48
  361.7 7.9 multiply_reduce_fusion.3
  369.8 4.2 multiply_reduce_fusion.2
  380.0 5.4 convolution_convert_fusion.2
  388.8 4.0 copy.250
  392.8 5.0 convolution_convert_fusion
  397.8 6.6 pad_maximum_fusion
  410.5 45.1 %all-gather.13.cloned.1.call-done = bf16[32,512,256]{2,1,0:T(8,128)(2,1)} async-done(((bf16[1,512,256]{2,1,0:T(8,128)(2,1)}), bf16[32,512,256]{2,1,0:T(8,128)(2,1)}) %all-gather.13.cloned.1.call-update) | async-done | bytes 8388624 | tf_op jit(solution)/shard_map/all_gather | solution.py:280
  455.6 5.3 multiply_reduce_fusion
  464.0 11.4 %while.39 = (s32[]{:T(128)}, f32[4,128,256]{2,1,0:T(8,128)S(1)}, f32[2,4,64,128]{3,2,0,1:T(8,128)}, f32[2,4,64,128]{3,2,0,1:T(8,128)}, f32[2,4,64,256]{3,2,0,1:T...) while((s32[]{:T(128)}, f32[4,128,256]{2,1,0:T(8,128)S(1)}, ...), condition=%wide.region_14.15_spmd, body=%wide.region_12.14_spmd.sunk | while | flops 403176960 | bytes 5259933 | solution.py:132
  484.3 4.4 reduce_window_sum.52
  497.3 5.2 multiply_reduce_fusion.4
  509.8 4.3 convolution_add_fusion.2
  514.2 87.6 %reduce-scatter.8.cloned.1.call-done = bf16[88,1024]{1,0:T(8,128)(2,1)} async-done(((bf16[2816,1024]{1,0:T(8,128)(2,1)}), bf16[88,1024]{1,0:T(8,128)(2,1)}) %reduce-scatter.8.cloned.1.call-update) | async-done | bytes 180240 | tf_op jit(solution)/shard_map/reduce_scatter | solution.py:309
  604.4 155.5 %reduce-scatter.6.cloned.1.call-done = bf16[32,6656]{1,0:T(8,128)(2,1)} async-done(((bf16[1024,6656]{1,0:T(8,128)(2,1)}), bf16[32,6656]{1,0:T(8,128)(2,1)}) %reduce-scatter.6.cloned.1.call-update) | async-done | bytes 426000 | tf_op jit(solution)/shard_map/reduce_scatter | solution.py:309
  763.3 144.0 %reduce-scatter.4.cloned.1.call-done = bf16[32,3328]{1,0:T(8,128)(2,1)} async-done(((bf16[1024,3328]{1,0:T(8,128)(2,1)}), bf16[32,3328]{1,0:T(8,128)(2,1)}) %reduce-scatter.4.cloned.1.call-update) | async-done | bytes 213008 | tf_op jit(solution)/shard_map/reduce_scatter | solution.py:309
  (264 shorter events, 111.1 us)
Async XLA Ops:
  7.2 82.2 %all-gather.7.cloned.1.call-start = ((), (), s32[]{:S(2)}) async-start(), calls=%async_computation.3 | async-start | bytes 7028736 | tf_op jit(solution)/shard_map/all_gather | solution.py:213
  15.5 169.3 %all-gather.15.cloned.1.call-start = ((), (), s32[]{:S(2)}) async-start(), calls=%async_computation.10 | async-start | bytes 8921088 | tf_op jit(solution)/shard_map/all_gather | solution.py:242
  16.7 80.8 %copy-start.39 = (f32[128]{0:T(128)}, f32[128]{0:T(128)S(1)}, u32[]{:S(2)}) copy-start(f32[128]{0:T(128)S(1)} %multiply_reduce_fusion.11) | copy-start | bytes 1540
  16.7 80.8 %copy-start.35 = (f32[128]{0:T(128)}, f32[128]{0:T(128)S(1)}, u32[]{:S(2)}) copy-start(f32[128]{0:T(128)S(1)} %fusion.114) | copy-start | bytes 1540
  103.4 8.3 copy-start.7
  107.2 87.7 %copy-start = (f32[2,4,64,128]{3,2,1,0:T(8,128)}, f32[2,4,64,128]{3,2,1,0:T(8,128)S(1)}, u32[]{:S(2)}) copy-start(f32[2,4,64,128]{3,2,1,0:T(8,128)S(1)} %get-tuple-element.871) | copy-start | bytes 786436
  108.0 178.3 %all-gather.9.cloned.1.call-start = ((), (), s32[]{:S(2)}) async-start(), calls=%async_computation.4 | async-start | bytes 14057472 | tf_op jit(solution)/shard_map/all_gather | solution.py:215
  109.9 244.9 %all-gather.11.cloned.1.call-start = ((), (), s32[]{:S(2)}) async-start(), calls=%async_computation.5 | async-start | bytes 5947392 | tf_op jit(solution)/shard_map/all_gather | solution.py:216
  110.5 345.1 %all-gather.13.cloned.1.call-start = ((), (), s32[]{:S(2)}) async-start(), calls=%async_computation.6 | async-start | bytes 8650752 | tf_op jit(solution)/shard_map/all_gather | solution.py:280
  113.0 82.7 %copy-start.18 = (f32[4,128,128]{2,1,0:T(8,128)S(1)}, f32[4,128,128]{2,1,0:T(8,128)}, u32[]{:S(2)}) copy-start(f32[4,128,128]{2,1,0:T(8,128)} %copy-done.17) | copy-start | bytes 786436
  186.4 9.9 %copy-start.4 = (f32[2,64,4,256]{3,2,1,0:T(4,128)S(1)}, f32[2,64,4,256]{3,2,1,0:T(4,128)}, u32[]{:S(2)}) copy-start(f32[2,64,4,256]{3,2,1,0:T(4,128)} %copy-done.3) | copy-start | bytes 1572868
  288.6 81.0 %copy-start.9 = (f32[128,1024]{1,0:T(8,128)}, f32[128,1024]{1,0:T(8,128)S(1)}, u32[]{:S(2)}) copy-start(f32[128,1024]{1,0:T(8,128)S(1)} %get-tuple-element.648) | copy-start | bytes 1572868
  361.7 7.9 copy-start.24
  361.7 8.1 copy-start.20
  361.7 8.1 copy-start.25
  379.8 222.0 %reduce-scatter.8.cloned.1.call-start = ((), (), s32[]{:S(2)}) async-start(), calls=%async_computation.9 | async-start | bytes 5947392 | tf_op jit(solution)/shard_map/reduce_scatter | solution.py:309
  385.5 374.4 %reduce-scatter.6.cloned.1.call-start = ((), (), s32[]{:S(2)}) async-start(), calls=%async_computation.8 | async-start | bytes 14057472 | tf_op jit(solution)/shard_map/reduce_scatter | solution.py:309
  404.4 502.9 %reduce-scatter.4.cloned.1.call-start = ((), (), s32[]{:S(2)}) async-start(), calls=%async_computation.7 | async-start | bytes 7028736 | tf_op jit(solution)/shard_map/reduce_scatter | solution.py:309
  475.5 7.9 copy-start.22
  475.5 7.9 copy-start.23
  480.4 15.4 %copy-start.26 = (f32[128,1024]{1,0:T(8,128)S(1)}, f32[128,1024]{1,0:T(8,128)}, u32[]{:S(2)}) copy-start(f32[128,1024]{1,0:T(8,128)} %get-tuple-element.616) | copy-start | bytes 1572868
  482.5 14.8 %copy-start.8 = (f32[128,1024]{1,0:T(8,128)S(1)}, f32[128,1024]{1,0:T(8,128)}, u32[]{:S(2)}) copy-start(f32[128,1024]{1,0:T(8,128)} %param.20) | copy-start | bytes 1572868
  508.6 94.9 %copy-start.40 = (f32[128]{0:T(128)S(1)}, f32[128]{0:T(128)}, u32[]{:S(2)}) copy-start(f32[128]{0:T(128)} %copy-done.39) | copy-start | bytes 1540
  508.6 94.9 %copy-start.16 = (f32[128,1024]{1,0:T(8,128)S(1)}, f32[128,1024]{1,0:T(8,128)}, u32[]{:S(2)}) copy-start(f32[128,1024]{1,0:T(8,128)} %copy-done.15) | copy-start | bytes 1572868
  (26 other events, 92.2 us)
Sparse Core Ops, SparseCore 0:
  15.6 73.6 all-gather.6
  108.2 76.5 all-gather.14
  187.6 98.6 all-gather.8
  289.0 65.8 all-gather.10
  379.9 75.6 all-gather.12
  457.8 143.9 reduce-scatter.7
  604.1 155.7 reduce-scatter.5
  762.2 145.0 reduce-scatter.3
